TPU v7x, 128 devices: a whole 4x4x4 slice. The times are simulated.
128 devices in a mesh: vocab: 32 (over z, x, core), tp: 4 (over y).
Axes of the slice: x: 4, y: 4, z: 4, core: 2. Of those that a mesh axis runs over, the one named last changes fastest.
Arguments:
- hidden: bfloat16 [16384, 2048], P('vocab'), may hold values from -28 to 28, as said below
- target_cluster: int32 [16384, 1], P('vocab'), may hold values from 0 to 255; in each aligned block of 512 rows (0 to 511, 512 to 1023, ...) at most 4 rows name the same one
- target_word: int32 [16384], P('vocab'), may hold values from 0 to 8191
- head_words: bfloat16 [2048, 8192], P(None, 'tp'), may hold values from -4 to 4
- head_clusters: bfloat16 [2048, 128], P(None, 'tp'), may hold values from -4 to 4
- proj_one: bfloat16 [32, 2048, 1024], P('vocab'), may hold values from -0.125 to 0.125
- proj_two: bfloat16 [32, 2048, 512], P('vocab'), may hold values from -0.125 to 0.125
- proj_three: bfloat16 [32, 2048, 256], P('vocab'), may hold values from -0.125 to 0.125
- proj_four: bfloat16 [32, 2048, 128], P('vocab'), may hold values from -0.125 to 0.125
- out_one: bfloat16 [32, 1024, 1024], P('vocab', None, 'tp'), may hold values from -4 to 4
- out_two: bfloat16 [32, 512, 2048], P('vocab', None, 'tp'), may hold values from -4 to 4
- out_three: bfloat16 [32, 256, 4096], P('vocab', None, 'tp'), may hold values from -4 to 4
- out_four: bfloat16 [32, 128, 8192], P('vocab', None, 'tp'), may hold values from -4 to 4
Outputs:
- grad_hidden: bfloat16 [16384, 2048], P('vocab', 'tp')
- grad_head_words: bfloat16 [2048, 8192], P('vocab', 'tp')
- grad_head_clusters: bfloat16 [2048, 128], P('vocab', 'tp')
- grad_proj_one: bfloat16 [32, 2048, 1024], P('vocab', 'tp')
- grad_proj_two: bfloat16 [32, 2048, 512], P('vocab', 'tp')
- grad_proj_three: bfloat16 [32, 2048, 256], P('vocab', 'tp')
- grad_proj_four: bfloat16 [32, 2048, 128], P('vocab', 'tp')
- grad_out_one: bfloat16 [32, 1024, 1024], P('vocab', None, 'tp')
- grad_out_two: bfloat16 [32, 512, 2048], P('vocab', None, 'tp')
- grad_out_three: bfloat16 [32, 256, 4096], P('vocab', None, 'tp')
- grad_out_four: bfloat16 [32, 128, 8192], P('vocab', None, 'tp')
Inputs may be any that keep to these rules, and one draw needn't show every extreme that they name: `hidden`: real values of order one, up to a factor that differs between tokens. `target_cluster`: A value below 128 names the tail cluster of the token's word; 128 or more marks a word of the head. Among the 512 tokens of one index of vocab no tail cluster is named more than 4 times. `target_word`: for a tail token only the value modulo its cluster's vocabulary counts.
All inputs are finite; a program needn't handle non-finite values.
Results may differ from a plain program's by a relative error of at most 0.017.
Values may be sent and summed in bfloat16 or wider, within the bound.
A program may use at most 128 MiB of HBM per device.

v0:
```python
import jax
import jax.numpy as jnp
from jax import lax
from jax.sharding import PartitionSpec as P


def sent_to_all(array, axis):
    copies = jnp.broadcast_to(array, (lax.axis_size(axis), *array.shape))
    return lax.all_to_all(copies, axis, split_axis=0, concat_axis=0, tiled=True)


def gathered_once(array, axis):
    leaves = jax.tree.leaves(array)
    order = sorted(range(len(leaves)), key=lambda k: -leaves[k].size)
    width = (1, *leaves[order[0]].shape)[-1]
    lines = [
        jnp.pad(leaves[k].reshape(-1), (0, -leaves[k].size % width)).reshape(-1, width)
        for k in order
    ]
    both, at, found = (sent_to_all(jnp.concatenate(lines), axis), 0, {})
    for k, line in zip(order, lines):
        share = both[:, at : at + len(line)].reshape(len(both), -1)
        found[k] = share[:, : leaves[k].size].reshape(-1, *leaves[k].shape)
        at += len(line)
    numbers = iter(range(len(leaves)))
    return jax.tree.map(lambda _: found[next(numbers)], array)


def combined_pairwise(pieces, combine):
    while len(jax.tree.leaves(pieces)[0]) > 1:
        pieces = jax.vmap(combine)(
            *(jax.tree.map(lambda part: part[side::2], pieces) for side in (0, 1))
        )
    return jax.tree.map(lambda part: part[0], pieces)


def merged(array, axis, combine):
    pieces = gathered_once(array, axis)
    return combined_pairwise(pieces, combine)


def split_up(array, dim, length):
    lengths = array.shape
    parts = array.reshape(*lengths[:dim], length, lengths[dim] // length, *lengths[dim + 1 :])
    return jnp.moveaxis(parts, dim, 0)


def sum_at_owner(array, axis, dim):
    parts = split_up(array, dim, lax.axis_size(axis))
    arrived = lax.all_to_all(parts, axis, split_axis=0, concat_axis=0, tiled=True)
    return arrived.astype(jnp.float32).sum(axis=0)


def of_everyone(array, axis):
    return sent_to_all(array, axis).astype(jnp.float32).sum(axis=0)


def online_pair(first, second):
    head_peak = jnp.maximum(first[0], second[0])
    head_total = first[1] * jnp.exp(first[0] - head_peak) + second[1] * jnp.exp(
        second[0] - head_peak
    )
    tail_peak = jnp.maximum(first[2], second[2])
    tail_total = first[3] * jnp.exp(first[2] - tail_peak) + second[3] * jnp.exp(
        second[2] - tail_peak
    )
    return (head_peak, head_total, tail_peak, tail_total)


def body(
    hidden,
    target_cluster,
    target_word,
    head_words,
    head_clusters,
    proj_one,
    proj_two,
    proj_three,
    proj_four,
    out_one,
    out_two,
    out_three,
    out_four,
):
    groups = lax.axis_size("vocab")
    splits = lax.axis_size("tp")
    tp_index = lax.axis_index("tp")
    tok_rows, width = hidden.shape
    capacity = tok_rows // (4 * groups)
    clusters = 4 * groups
    slots = groups * capacity
    word_cols = head_words.shape[1]
    clus_cols = head_clusters.shape[1]
    own_width = width // splits
    logit_words = jnp.dot(hidden, head_words, preferred_element_type=jnp.float32)
    logit_clus = jnp.dot(hidden, head_clusters, preferred_element_type=jnp.float32)
    head_peak = jnp.maximum(jnp.max(logit_words, axis=1), jnp.max(logit_clus, axis=1))
    head_total = jnp.sum(jnp.exp(logit_words - head_peak[:, None]), axis=1) + jnp.sum(
        jnp.exp(logit_clus - head_peak[:, None]), axis=1
    )
    cluster_ids = target_cluster[:, 0]
    tail_mask = cluster_ids < clusters
    band_ids = cluster_ids // groups
    owner_ids = cluster_ids % groups
    member = (cluster_ids[:, None] == jnp.arange(clusters, dtype=jnp.int32)[None, :]).astype(
        jnp.int32
    )
    rank = jnp.sum((jnp.cumsum(member, axis=0) - 1) * member, axis=1)
    flat = jnp.where(tail_mask, owner_ids * 4 * capacity + band_ids * capacity + rank, -1)
    dispatch = jnp.arange(tok_rows, dtype=jnp.int32)[:, None] == flat[None, :]
    dispatch_bf = dispatch.astype(jnp.bfloat16)
    send_rows = jnp.dot(dispatch_bf, hidden, preferred_element_type=jnp.float32).astype(
        jnp.bfloat16
    )
    send_words = jnp.sum(dispatch.astype(jnp.int32) * (target_word + 1)[None, :], axis=1) - 1
    recv_rows, recv_words = (
        lax.all_to_all(
            send_rows.reshape(groups, 4 * capacity, width),
            "vocab",
            split_axis=0,
            concat_axis=0,
            tiled=True,
        ),
        lax.all_to_all(
            send_words.reshape(groups, 4 * capacity),
            "vocab",
            split_axis=0,
            concat_axis=0,
            tiled=True,
        ),
    )
    projections = (proj_one, proj_two, proj_three, proj_four)
    outputs = (out_one, out_two, out_three, out_four)
    band_rows = []
    band_valid = []
    band_local = []
    band_reduced = []
    band_logits = []
    for band in range(4):
        rows = recv_rows[:, band * capacity : (band + 1) * capacity, :].reshape(slots, width)
        words = recv_words[:, band * capacity : (band + 1) * capacity].reshape(slots)
        weight_out = outputs[band][0]
        vcols = weight_out.shape[1]
        valid = words >= 0
        local = jnp.where(valid, words % (vcols * splits) - tp_index * vcols, -1)
        reduced = jnp.dot(rows, projections[band][0], preferred_element_type=jnp.float32).astype(
            jnp.bfloat16
        )
        logits = jnp.dot(reduced, weight_out, preferred_element_type=jnp.float32)
        band_rows.append(rows)
        band_valid.append(valid)
        band_local.append(local)
        band_reduced.append(reduced)
        band_logits.append(logits)
    tail_peak = jnp.stack([jnp.max(logits, axis=1) for logits in band_logits])
    tail_total = jnp.stack(
        [
            jnp.sum(jnp.exp(band_logits[band] - tail_peak[band][:, None]), axis=1)
            for band in range(4)
        ]
    )
    head_peak, head_total, tail_peak, tail_total = merged(
        (head_peak, head_total, tail_peak, tail_total), "tp", online_pair
    )
    word_target = jnp.where(tail_mask, -1, target_word - tp_index * word_cols)
    clus_target = jnp.where(tail_mask, cluster_ids - tp_index * clus_cols, -1)
    inverse = 1.0 / head_total
    probs_words = jnp.exp(logit_words - head_peak[:, None]) * inverse[:, None]
    probs_clus = jnp.exp(logit_clus - head_peak[:, None]) * inverse[:, None]
    hit_words = (jnp.arange(word_cols, dtype=jnp.int32)[None, :] == word_target[:, None]).astype(
        jnp.float32
    )
    hit_clus = (jnp.arange(clus_cols, dtype=jnp.int32)[None, :] == clus_target[:, None]).astype(
        jnp.float32
    )
    grad_words = (probs_words - hit_words).astype(jnp.bfloat16)
    grad_clus = (probs_clus - hit_clus).astype(jnp.bfloat16)
    head_part = jnp.dot(grad_words, head_words.T, preferred_element_type=jnp.float32) + jnp.dot(
        grad_clus, head_clusters.T, preferred_element_type=jnp.float32
    )
    head_mine = sum_at_owner(head_part.astype(jnp.bfloat16), "tp", 1)
    band_dlog = []
    partials = []
    for band in range(4):
        weight_out = outputs[band][0]
        vcols = weight_out.shape[1]
        probs = jnp.exp(band_logits[band] - tail_peak[band][:, None]) / tail_total[band][:, None]
        hit = (jnp.arange(vcols, dtype=jnp.int32)[None, :] == band_local[band][:, None]).astype(
            jnp.float32
        )
        dlog = ((probs - hit) * band_valid[band][:, None].astype(jnp.float32)).astype(jnp.bfloat16)
        band_dlog.append(dlog)
        partials.append(jnp.dot(dlog, weight_out.T, preferred_element_type=jnp.float32))
    summed = (
        of_everyone(partials[0].astype(jnp.bfloat16), "tp").astype(jnp.float32),
        of_everyone(partials[1].astype(jnp.bfloat16), "tp").astype(jnp.float32),
        of_everyone(partials[2].astype(jnp.bfloat16), "tp").astype(jnp.float32),
        of_everyone(partials[3].astype(jnp.bfloat16), "tp").astype(jnp.float32),
    )
    grads_out = []
    grads_proj = []
    backs = []
    for band in range(4):
        dred = summed[band].astype(jnp.bfloat16)
        weight_in = projections[band][0]
        grads_out.append(
            jnp.dot(
                band_reduced[band].T, band_dlog[band], preferred_element_type=jnp.float32
            ).astype(jnp.bfloat16)[None]
        )
        rows_mine = lax.dynamic_slice_in_dim(band_rows[band], tp_index * own_width, own_width, 1)
        grads_proj.append(
            jnp.dot(rows_mine.T, dred, preferred_element_type=jnp.float32).astype(jnp.bfloat16)[
                None
            ]
        )
        weight_mine = lax.dynamic_slice_in_dim(weight_in, tp_index * own_width, own_width, 0)
        back = jnp.dot(dred, weight_mine.T, preferred_element_type=jnp.float32).astype(jnp.bfloat16)
        backs.append(back.reshape(groups, capacity, back.shape[1]))
    back_all = jnp.concatenate(backs, axis=1)
    returned = lax.all_to_all(back_all, "vocab", split_axis=0, concat_axis=0, tiled=True).reshape(
        tok_rows, back_all.shape[2]
    )
    tail_part = jnp.dot(dispatch_bf.T, returned, preferred_element_type=jnp.float32)
    grad_hidden = (head_mine + tail_part).astype(jnp.bfloat16)
    grads_cat = jnp.concatenate([grad_words, grad_clus], axis=1)
    head_sum = lax.psum_scatter(
        jnp.dot(hidden.T, grads_cat, preferred_element_type=jnp.float32).astype(jnp.bfloat16),
        "vocab",
        scatter_dimension=0,
        tiled=True,
    ).astype(jnp.float32)
    grad_head_words = head_sum[:, :word_cols].astype(jnp.bfloat16)
    grad_head_clusters = head_sum[:, word_cols:].astype(jnp.bfloat16)
    return (
        grad_hidden,
        grad_head_words,
        grad_head_clusters,
        grads_proj[0],
        grads_proj[1],
        grads_proj[2],
        grads_proj[3],
        grads_out[0],
        grads_out[1],
        grads_out[2],
        grads_out[3],
    )


def solution(mesh):
    return jax.shard_map(
        body,
        mesh=mesh,
        in_specs=(
            P("vocab", None),
            P("vocab", None),
            P("vocab"),
            P(None, "tp"),
            P(None, "tp"),
            P("vocab", None, None),
            P("vocab", None, None),
            P("vocab", None, None),
            P("vocab", None, None),
            P("vocab", None, "tp"),
            P("vocab", None, "tp"),
            P("vocab", None, "tp"),
            P("vocab", None, "tp"),
        ),
        out_specs=(
            P("vocab", "tp"),
            P("vocab", "tp"),
            P("vocab", "tp"),
            P("vocab", "tp", None),
            P("vocab", "tp", None),
            P("vocab", "tp", None),
            P("vocab", "tp", None),
            P("vocab", None, "tp"),
            P("vocab", None, "tp"),
            P("vocab", None, "tp"),
            P("vocab", None, "tp"),
        ),
        check_vma=False,
    )
```

profile of v0, /device:TPU:1, one launch (start us, length us, event | category | flops | bytes accessed | tf_op | source)
XLA Modules:
  0.0 228.7 jit_solution(14207189033129298444)
XLA Ops:
  10.1 2.6 %convolution_convert_fusion.1 = bf16[512,2048]{1,0:T(8,128)(2,1)} fusion(bf16[512,2048]{1,0:T(8,128)(2,1)S(1)} %copy-done, s32[512]{0:T(512)S(1)} %get-tuple-element.96), kind=kOutput, calls=%fused_computation.9 | convolution fusion | flops 1075052544 | bytes 4196352 | tf_op jit(solution)/shard_map/dot_general | solution.py:112
  12.8 9.6 %all-to-all-start = ((bf16[32,16,2048]{2,1,0:T(8,128)(2,1)}), bf16[32,16,2048]{2,1,0:T(8,128)(2,1)}, u32[]{:S(2)}, u32[]{:S(2)}) async-start(bf16[32,16,2048]{2,1,0:T(8,128)(2,1)} %bitcast.170), calls=%async_computation | async-start | bytes 4194304 | tf_op jit(solution)/shard_map/all_to_all | solution.py:117
  23.1 7.0 %fusion.89 = (f32[512]{0:T(512)S(1)}, f32[512,2048]{1,0:T(8,128)S(1)}) fusion(bf16[512,2048]{1,0:T(8,128)(2,1)S(1)} %copy-done, bf16[2048,2048]{1,0:T(8,128)(2,1)} %param.16), kind=kOutput, calls=%fused_computation.188 | convolution fusion | flops 4296015360 | bytes 14682112 | tf_op jit(solution)/shard_map/dot_general | solution.py:95
  30.2 1.9 copy-done.2
  32.8 17.4 %all-to-all-done = bf16[32,16,2048]{2,1,0:T(8,128)(2,1)} async-done(((bf16[32,16,2048]{2,1,0:T(8,128)(2,1)}), bf16[32,16,2048]{2,1,0:T(8,128)(2,1)}, u32[]{:S(2)}, u32[]{:S(2)}) %all-to-all-start) | async-done | bytes 2097184 | tf_op jit(solution)/shard_map/all_to_all | solution.py:117
  50.3 4.3 %fusion.82 = (bf16[32,4,2048]{2,1,0:T(4,128)(2,1)}, bf16[32,4,2048]{2,1,0:T(4,128)(2,1)S(1)}, bf16[32,4,2048]{2,1,0:T(4,128)(2,1)}, bf16[32,4,2048]{2,1,0:T(4,128)(2,1)}) fusion(bf16[32,16,2048]{2,1,0:T(8,128)(2,1)} %all-to-all-done), kind=kLoop, calls=%fused_computation.181 | loop fusion | bytes 4194304 | tf_op jit(solution)/shard_map/slice | solution.py:140
  57.9 2.1 reshape.380
  60.0 3.1 %fusion.15 = bf16[128,1024]{1,0:T(8,128)(2,1)S(1)} fusion(bf16[128,2048]{1,0:T(8,128)(2,1)S(1)} %reshape.379, bf16[1,2048,1024]{2,1,0:T(8,128)(2,1)} %param.18), kind=kOutput, calls=%fused_computation.32 | convolution fusion | flops 537001984 | bytes 4980736 | tf_op jit(solution)/shard_map/dot_general | solution.py:146
  69.2 4.2 %all-to-all-start.1 = ((f32[4,4,512]{2,1,0:T(4,128)}), f32[4,4,512]{2,1,0:T(4,128)S(1)}, u32[]{:S(2)}, u32[]{:S(2)}) async-start(f32[4,4,512]{2,1,0:T(4,128)} %broadcast_in_dim.40), calls=%async_computation.1 | async-start | bytes 65536 | tf_op jit(solution)/shard_map/all_to_all | solution.py:9
  73.4 4.3 %all-to-all-done.1 = f32[4,4,512]{2,1,0:T(4,128)S(1)} async-done(((f32[4,4,512]{2,1,0:T(4,128)}), f32[4,4,512]{2,1,0:T(4,128)S(1)}, u32[]{:S(2)}, u32[]{:S(2)}) %all-to-all-start.1) | async-done | bytes 32800 | tf_op jit(solution)/shard_map/all_to_all | solution.py:9
  77.9 4.7 %subtract_convert_fusion = bf16[512,2048]{1,0:T(8,128)(2,1)} fusion(f32[512,2048]{1,0:T(8,128)} %copy-done.2, s32[512]{0:T(512)S(1)} %get-tuple-element.95, f32[512]{0:T(512)S(1)} %bitcast.178, f32[512]{0:T(512)S(1)} %bitcast.180), kind=kLoop, calls=%fused_computation.6 | loop fusion | flops 6291456 | bytes 6297600 | tf_op jit(solution)/shard_map/convert_element_type | solution.py:176
  82.8 8.5 %fusion = bf16[2048,2080]{0,1:T(8,128)(2,1)} fusion(bf16[512,2048]{1,0:T(8,128)(2,1)S(1)} %copy-done, bf16[512,32]{1,0:T(8,128)(2,1)S(1)} %copy.50, bf16[512,2048]{1,0:T(8,128)(2,1)} %subtract_convert_fusion), kind=kOutput, calls=%fused_computation.1 | convolution fusion | flops 4370595840 | bytes 12746752 | tf_op jit(solution)/shard_map/dot_general | solution.py:228
  91.3 11.8 %copy.52 = bf16[2048,2080]{1,0:T(8,128)(2,1)} copy(bf16[2048,2080]{0,1:T(8,128)(2,1)} %fusion) | data formatting | bytes 17039360
  104.0 7.3 %all-to-all-start.3 = ((s32[32,1,16]{2,1,0:T(1,128)}), s32[32,1,16]{2,1,0:T(1,128)S(1)}, u32[]{:S(2)}, u32[]{:S(2)}) async-start(s32[32,1,16]{2,1,0:T(1,128)} %bitcast.35), calls=%async_computation.3 | async-start | bytes 32768 | tf_op jit(solution)/shard_map/all_to_all | solution.py:124
  111.3 7.0 %all-to-all-done.3 = s32[32,1,16]{2,1,0:T(1,128)S(1)} async-done(((s32[32,1,16]{2,1,0:T(1,128)}), s32[32,1,16]{2,1,0:T(1,128)S(1)}, u32[]{:S(2)}, u32[]{:S(2)}) %all-to-all-start.3) | async-done | bytes 2080 | tf_op jit(solution)/shard_map/all_to_all | solution.py:124
  123.3 3.3 %all-to-all-start.7 = ((bf16[4,128,128]{2,1,0:T(8,128)(2,1)}), bf16[4,128,128]{2,1,0:T(8,128)(2,1)S(1)}, u32[]{:S(2)}, u32[]{:S(2)}) async-start(bf16[4,128,128]{2,1,0:T(8,128)(2,1)} %broadcast_in_dim.83), calls=%async_computation.7 | async-start | bytes 262144 | tf_op jit(solution)/shard_map/all_to_all | solution.py:9
  127.8 3.5 %all-to-all-done.7 = bf16[4,128,128]{2,1,0:T(8,128)(2,1)S(1)} async-done(((bf16[4,128,128]{2,1,0:T(8,128)(2,1)}), bf16[4,128,128]{2,1,0:T(8,128)(2,1)S(1)}, u32[]{:S(2)}, u32[]{:S(2)}) %all-to-all-start.7) | async-done | bytes 131104 | tf_op jit(solution)/shard_map/all_to_all | solution.py:9
  132.1 3.4 %all-to-all-start.6 = ((bf16[4,128,256]{2,1,0:T(8,128)(2,1)}), bf16[4,128,256]{2,1,0:T(8,128)(2,1)S(1)}, u32[]{:S(2)}, u32[]{:S(2)}) async-start(bf16[4,128,256]{2,1,0:T(8,128)(2,1)} %broadcast_in_dim.82), calls=%async_computation.6 | async-start | bytes 524288 | tf_op jit(solution)/shard_map/all_to_all | solution.py:9
  137.1 4.0 %all-to-all-done.6 = bf16[4,128,256]{2,1,0:T(8,128)(2,1)S(1)} async-done(((bf16[4,128,256]{2,1,0:T(8,128)(2,1)}), bf16[4,128,256]{2,1,0:T(8,128)(2,1)S(1)}, u32[]{:S(2)}, u32[]{:S(2)}) %all-to-all-start.6) | async-done | bytes 262176 | tf_op jit(solution)/shard_map/all_to_all | solution.py:9
  141.9 3.5 %all-to-all-start.5 = ((bf16[4,128,512]{2,1,0:T(8,128)(2,1)}), bf16[4,128,512]{2,1,0:T(8,128)(2,1)S(1)}, u32[]{:S(2)}, u32[]{:S(2)}) async-start(bf16[4,128,512]{2,1,0:T(8,128)(2,1)} %broadcast_in_dim.81), calls=%async_computation.5 | async-start | bytes 1048576 | tf_op jit(solution)/shard_map/all_to_all | solution.py:9
  145.8 6.5 %all-to-all-done.5 = bf16[4,128,512]{2,1,0:T(8,128)(2,1)S(1)} async-done(((bf16[4,128,512]{2,1,0:T(8,128)(2,1)}), bf16[4,128,512]{2,1,0:T(8,128)(2,1)S(1)}, u32[]{:S(2)}, u32[]{:S(2)}) %all-to-all-start.5) | async-done | bytes 524320 | tf_op jit(solution)/shard_map/all_to_all | solution.py:9
  153.4 3.5 %all-to-all-start.4 = ((bf16[4,128,1024]{2,1,0:T(8,128)(2,1)}), bf16[4,128,1024]{2,1,0:T(8,128)(2,1)S(1)}, u32[]{:S(2)}, u32[]{:S(2)}) async-start(bf16[4,128,1024]{2,1,0:T(8,128)(2,1)} %broadcast_in_dim.80), calls=%async_computation.4 | async-start | bytes 2097152 | tf_op jit(solution)/shard_map/all_to_all | solution.py:9
  157.0 7.8 %fusion.91 = f32[512,2048]{1,0:T(8,128)S(1)} fusion(bf16[512,2048]{1,0:T(8,128)(2,1)} %subtract_convert_fusion, bf16[2048,2048]{1,0:T(8,128)(2,1)} %param.16), kind=kOutput, calls=%fused_computation.190 | convolution fusion | flops 4294967296 | bytes 14680064 | tf_op jit(solution)/shard_map/dot_general | solution.py:178
  168.4 4.8 %all-to-all-start.2 = ((bf16[4,512,512]{2,1,0:T(8,128)(2,1)}), bf16[4,512,512]{2,1,0:T(8,128)(2,1)}, u32[]{:S(2)}, u32[]{:S(2)}) async-start(bf16[4,512,512]{2,1,0:T(8,128)(2,1)} %bitcast.169), calls=%async_computation.2 | async-start | bytes 4194304 | tf_op jit(solution)/shard_map/all_to_all | solution.py:50
  185.8 9.5 %all-to-all-done.2 = bf16[4,512,512]{2,1,0:T(8,128)(2,1)} async-done(((bf16[4,512,512]{2,1,0:T(8,128)(2,1)}), bf16[4,512,512]{2,1,0:T(8,128)(2,1)}, u32[]{:S(2)}, u32[]{:S(2)}) %all-to-all-start.2) | async-done | bytes 2097184 | tf_op jit(solution)/shard_map/all_to_all | solution.py:50
  195.2 9.5 %all-to-all-start.8 = ((bf16[32,16,512]{2,1,0:T(8,128)(2,1)}), bf16[32,16,512]{2,1,0:T(8,128)(2,1)}, u32[]{:S(2)}, u32[]{:S(2)}) async-start(bf16[32,16,512]{2,1,0:T(8,128)(2,1)} %pad_maximum_fusion), calls=%async_computation.8 | async-start | bytes 1048576 | tf_op jit(solution)/shard_map/all_to_all | solution.py:221
  204.8 2.0 fusion.18
  206.8 2.0 fusion.11
  208.8 2.3 %fusion.9 = bf16[1,512,1024]{2,1,0:T(8,128)(2,1)} fusion(bf16[128,1024]{1,0:T(8,128)(2,1)S(1)} %reduce_sum.138, bf16[128,2048]{1,0:T(8,128)(2,1)} %copy-done.8, s32[]{:T(128)S(6)} %select_n.116), kind=kOutput, calls=%fused_computation.19 | convolution fusion | flops 134742016 | bytes 1441796 | tf_op jit(solution)/shard_map/dot_general | solution.py:213
  211.1 2.0 convert_reduce_fusion
  213.1 3.3 %all-to-all-done.8 = bf16[32,16,512]{2,1,0:T(8,128)(2,1)} async-done(((bf16[32,16,512]{2,1,0:T(8,128)(2,1)}), bf16[32,16,512]{2,1,0:T(8,128)(2,1)}, u32[]{:S(2)}, u32[]{:S(2)}) %all-to-all-start.8) | async-done | bytes 524320 | tf_op jit(solution)/shard_map/all_to_all | solution.py:221
  216.5 2.3 %fusion.10 = bf16[512,512]{1,0:T(8,128)(2,1)} fusion(f32[512,512]{1,0:T(8,128)S(1)} %convert_reduce_fusion, bf16[512,512]{1,0:T(8,128)(2,1)} %bitcast.47, s32[512]{0:T(512)S(1)} %get-tuple-element.96), kind=kOutput, calls=%fused_computation.21 | convolution fusion | flops 269221888 | bytes 2099200 | tf_op jit(solution)/shard_map/dot_general | solution.py:224
  (198 shorter events, 44.6 us)
Async XLA Ops:
  12.8 9.6 %copy-start.34 = (bf16[2048,32]{0,1:T(8,128)(2,1)S(1)}, bf16[2048,32]{0,1:T(8,128)(2,1)}, u32[]{:S(2)}) copy-start(bf16[2048,32]{0,1:T(8,128)(2,1)} %param.17) | copy-start | bytes 393220
  12.8 37.5 %all-to-all-start = ((bf16[32,16,2048]{2,1,0:T(8,128)(2,1)}), bf16[32,16,2048]{2,1,0:T(8,128)(2,1)}, u32[]{:S(2)}, u32[]{:S(2)}) async-start(bf16[32,16,2048]{2,1,0:T(8,128)(2,1)} %bitcast.170), calls=%async_computation | async-start | bytes 4194304 | tf_op jit(solution)/shard_map/all_to_all | solution.py:117
  55.7 8.9 %copy-start.8 = (bf16[128,2048]{1,0:T(8,128)(2,1)}, bf16[128,2048]{1,0:T(8,128)(2,1)S(1)}, u32[]{:S(2)}) copy-start(bf16[128,2048]{1,0:T(8,128)(2,1)S(1)} %reshape.379) | copy-start | bytes 1572868
  65.9 16.7 %copy-start.36 = (bf16[128,512]{1,0:T(8,128)(2,1)}, bf16[128,512]{1,0:T(8,128)(2,1)S(1)}, u32[]{:S(2)}) copy-start(bf16[128,512]{1,0:T(8,128)(2,1)S(1)} %fusion.19) | copy-start | bytes 393220
  69.2 8.5 %all-to-all-start.1 = ((f32[4,4,512]{2,1,0:T(4,128)}), f32[4,4,512]{2,1,0:T(4,128)S(1)}, u32[]{:S(2)}, u32[]{:S(2)}) async-start(f32[4,4,512]{2,1,0:T(4,128)} %broadcast_in_dim.40), calls=%async_computation.1 | async-start | bytes 65536 | tf_op jit(solution)/shard_map/all_to_all | solution.py:9
  73.4 145.4 %reduce-scatter.4.cloned.1.call-start = ((), (), s32[]{:S(2)}) async-start(), calls=%async_computation.10 | async-start | bytes 9191424
  103.1 19.1 %copy-start.13 = (bf16[1,128,2048]{2,1,0:T(8,128)(2,1)S(1)}, bf16[1,128,2048]{2,1,0:T(8,128)(2,1)}, u32[]{:S(2)}) copy-start(bf16[1,128,2048]{2,1,0:T(8,128)(2,1)} %param.25) | copy-start | bytes 1572868
  103.1 23.5 %copy-start.4 = (f32[128,1024]{1,0:T(8,128)S(1)}, f32[128,1024]{1,0:T(8,128)}, u32[]{:S(2)}) copy-start(f32[128,1024]{1,0:T(8,128)} %copy-done.3) | copy-start | bytes 1572868
  103.1 24.4 %copy-start.15 = (bf16[1,256,1024]{2,1,0:T(8,128)(2,1)S(1)}, bf16[1,256,1024]{2,1,0:T(8,128)(2,1)}, u32[]{:S(2)}) copy-start(bf16[1,256,1024]{2,1,0:T(8,128)(2,1)} %param.24) | copy-start | bytes 1572868
  104.0 14.3 %all-to-all-start.3 = ((s32[32,1,16]{2,1,0:T(1,128)}), s32[32,1,16]{2,1,0:T(1,128)S(1)}, u32[]{:S(2)}, u32[]{:S(2)}) async-start(s32[32,1,16]{2,1,0:T(1,128)} %bitcast.35), calls=%async_computation.3 | async-start | bytes 32768 | tf_op jit(solution)/shard_map/all_to_all | solution.py:124
  122.2 23.6 %copy-start.5 = (bf16[128,2048]{1,0:T(8,128)(2,1)}, bf16[128,2048]{1,0:T(8,128)(2,1)S(1)}, u32[]{:S(2)}) copy-start(bf16[128,2048]{1,0:T(8,128)(2,1)S(1)} %multiply_convert_fusion) | copy-start | bytes 1572868
  122.2 23.2 %copy-start.28 = (f32[128,256]{1,0:T(8,128)S(1)}, f32[128,256]{1,0:T(8,128)}, u32[]{:S(2)}) copy-start(f32[128,256]{1,0:T(8,128)} %copy-done.27) | copy-start | bytes 393220
  122.2 23.2 %copy-start.33 = (bf16[1,1024,256]{2,1,0:T(8,128)(2,1)S(1)}, bf16[1,1024,256]{2,1,0:T(8,128)(2,1)}, u32[]{:S(2)}) copy-start(bf16[1,1024,256]{2,1,0:T(8,128)(2,1)} %param.22) | copy-start | bytes 1572868
  122.2 23.2 %copy-start.43 = (f32[128]{0:T(128)S(1)}, f32[128]{0:T(128)}, u32[]{:S(2)}) copy-start(f32[128]{0:T(128)} %get-tuple-element.90) | copy-start | bytes 1540
  122.3 23.2 %copy-start.45 = (f32[128]{0:T(128)S(1)}, f32[128]{0:T(128)}, u32[]{:S(2)}) copy-start(f32[128]{0:T(128)} %get-tuple-element.118) | copy-start | bytes 1540
  122.3 23.2 %copy-start.49 = (f32[128]{0:T(128)S(1)}, f32[128]{0:T(128)}, u32[]{:S(2)}) copy-start(f32[128]{0:T(128)} %compare_convert_fusion.3) | copy-start | bytes 1540
  123.3 8.1 %all-to-all-start.7 = ((bf16[4,128,128]{2,1,0:T(8,128)(2,1)}), bf16[4,128,128]{2,1,0:T(8,128)(2,1)S(1)}, u32[]{:S(2)}, u32[]{:S(2)}) async-start(bf16[4,128,128]{2,1,0:T(8,128)(2,1)} %broadcast_in_dim.83), calls=%async_computation.7 | async-start | bytes 262144 | tf_op jit(solution)/shard_map/all_to_all | solution.py:9
  126.6 18.8 %copy-start.42 = (s32[128]{0:T(128)S(1)}, s32[128]{0:T(128)}, u32[]{:S(2)}) copy-start(s32[128]{0:T(128)} %copy-done.41) | copy-start | bytes 1540
  131.4 22.1 %copy-start.30 = (bf16[4,128,128]{2,1,0:T(8,128)(2,1)}, bf16[4,128,128]{2,1,0:T(8,128)(2,1)S(1)}, u32[]{:S(2)}) copy-start(bf16[4,128,128]{2,1,0:T(8,128)(2,1)S(1)} %all-to-all-done.7) | copy-start | bytes 393220
  132.1 8.9 %all-to-all-start.6 = ((bf16[4,128,256]{2,1,0:T(8,128)(2,1)}), bf16[4,128,256]{2,1,0:T(8,128)(2,1)S(1)}, u32[]{:S(2)}, u32[]{:S(2)}) async-start(bf16[4,128,256]{2,1,0:T(8,128)(2,1)} %broadcast_in_dim.82), calls=%async_computation.6 | async-start | bytes 524288 | tf_op jit(solution)/shard_map/all_to_all | solution.py:9
  141.9 10.4 %all-to-all-start.5 = ((bf16[4,128,512]{2,1,0:T(8,128)(2,1)}), bf16[4,128,512]{2,1,0:T(8,128)(2,1)S(1)}, u32[]{:S(2)}, u32[]{:S(2)}) async-start(bf16[4,128,512]{2,1,0:T(8,128)(2,1)} %broadcast_in_dim.81), calls=%async_computation.5 | async-start | bytes 1048576 | tf_op jit(solution)/shard_map/all_to_all | solution.py:9
  153.4 15.0 %all-to-all-start.4 = ((bf16[4,128,1024]{2,1,0:T(8,128)(2,1)}), bf16[4,128,1024]{2,1,0:T(8,128)(2,1)S(1)}, u32[]{:S(2)}, u32[]{:S(2)}) async-start(bf16[4,128,1024]{2,1,0:T(8,128)(2,1)} %broadcast_in_dim.80), calls=%async_computation.4 | async-start | bytes 2097152 | tf_op jit(solution)/shard_map/all_to_all | solution.py:9
  165.6 8.8 %copy-start.44 = (f32[128]{0:T(128)S(1)}, f32[128]{0:T(128)}, u32[]{:S(2)}) copy-start(f32[128]{0:T(128)} %get-tuple-element.90) | copy-start | bytes 1540
  165.6 8.8 %copy-start.46 = (f32[128]{0:T(128)S(1)}, f32[128]{0:T(128)}, u32[]{:S(2)}) copy-start(f32[128]{0:T(128)} %get-tuple-element.118) | copy-start | bytes 1540
  165.6 8.8 %copy-start.50 = (f32[128]{0:T(128)S(1)}, f32[128]{0:T(128)}, u32[]{:S(2)}) copy-start(f32[128]{0:T(128)} %compare_convert_fusion.3) | copy-start | bytes 1540
  167.2 8.4 %copy-start.22 = (f32[128,512]{1,0:T(8,128)S(1)}, f32[128,512]{1,0:T(8,128)}, u32[]{:S(2)}) copy-start(f32[128,512]{1,0:T(8,128)} %copy-done.21) | copy-start | bytes 786436
  167.3 9.5 %copy-start.31 = (bf16[4,128,128]{2,1,0:T(8,128)(2,1)S(1)}, bf16[4,128,128]{2,1,0:T(8,128)(2,1)}, u32[]{:S(2)}) copy-start(bf16[4,128,128]{2,1,0:T(8,128)(2,1)} %copy-done.30) | copy-start | bytes 393220
  168.4 11.4 %copy-start.24 = (bf16[4,128,256]{2,1,0:T(8,128)(2,1)S(1)}, bf16[4,128,256]{2,1,0:T(8,128)(2,1)}, u32[]{:S(2)}) copy-start(bf16[4,128,256]{2,1,0:T(8,128)(2,1)} %copy-done.23) | copy-start | bytes 786436
  168.4 12.7 %copy-start.17 = (bf16[4,128,512]{2,1,0:T(8,128)(2,1)S(1)}, bf16[4,128,512]{2,1,0:T(8,128)(2,1)}, u32[]{:S(2)}) copy-start(bf16[4,128,512]{2,1,0:T(8,128)(2,1)} %copy-done.16) | copy-start | bytes 1572868
  168.4 26.8 %all-to-all-start.2 = ((bf16[4,512,512]{2,1,0:T(8,128)(2,1)}), bf16[4,512,512]{2,1,0:T(8,128)(2,1)}, u32[]{:S(2)}, u32[]{:S(2)}) async-start(bf16[4,512,512]{2,1,0:T(8,128)(2,1)} %bitcast.169), calls=%async_computation.2 | async-start | bytes 4194304 | tf_op jit(solution)/shard_map/all_to_all | solution.py:50
  195.2 21.2 %all-to-all-start.8 = ((bf16[32,16,512]{2,1,0:T(8,128)(2,1)}), bf16[32,16,512]{2,1,0:T(8,128)(2,1)}, u32[]{:S(2)}, u32[]{:S(2)}) async-start(bf16[32,16,512]{2,1,0:T(8,128)(2,1)} %pad_maximum_fusion), calls=%async_computation.8 | async-start | bytes 1048576 | tf_op jit(solution)/shard_map/all_to_all | solution.py:221
  204.7 17.1 %copy-start.1 = (bf16[512,2048]{1,0:T(8,128)(2,1)S(1)}, bf16[512,2048]{1,0:T(8,128)(2,1)}, u32[]{:S(2)}) copy-start(bf16[512,2048]{1,0:T(8,128)(2,1)} %param.13) | copy-start | bytes 6291460
  (29 other events, 146.9 us)
Sparse Core Ops, SparseCore 0:
  103.2 90.8 reduce-scatter.3
where the time goes:
time: 230 us; the launch traced here: 229 us
  matrix products  57 us (25%)
  waiting for transfers between devices  55.5 us (24%)
  starting transfers between devices  49.1 us (21%)
  local copies, waits for them, and re-layouts  36.3 us (16%)
  other arithmetic  15.8 us (7%)
  between operations  15 us (7%)
    all_to_all x5, waiting for transfers between devices, sent_to_all(): return lax.all_to_all(copies, axis, split_axis=0, concat_axis=0, tiled=True)  18.3 us
    all_to_all x5, starting transfers between devices, sent_to_all(): return lax.all_to_all(copies, axis, split_axis=0, concat_axis=0, tiled=True)  17.9 us
    all_to_all x1, waiting for transfers between devices, body(): lax.all_to_all(send_rows.reshape(groups, 4 * capacity, width), 'vocab', s...  17.4 us
    unnamed x104, local copies, waits for them, and re-layouts  15.4 us
    all_to_all x1, starting transfers between devices, body(): lax.all_to_all(send_rows.reshape(groups, 4 * capacity, width), 'vocab', s...  9.61 us
    all_to_all x1, starting transfers between devices, body(): lax.all_to_all(back_all, 'vocab', split_axis=0, concat_axis=0, tiled=True)  9.49 us
    all_to_all x1, waiting for transfers between devices, sum_at_owner(): lax.all_to_all(parts, axis, split_axis=0, concat_axis=0, tiled=True)  9.46 us
    dot_general x1, matrix products, body(): jnp.dot(hidden.T, grads_cat, preferred_element_type=jnp.float32)  8.52 us
  transfers between devices with their start and end apart: 10, of which 8 were waited for; matrix products, arithmetic and copies ran while one was open for 24% of the time, Pallas kernels for 0%

commit v1 on v0

--- a/solution.py
+++ b/solution.py
@@ -102,10 +102,9 @@
     tail_mask = cluster_ids < clusters
     band_ids = cluster_ids // groups
     owner_ids = cluster_ids % groups
-    member = (cluster_ids[:, None] == jnp.arange(clusters, dtype=jnp.int32)[None, :]).astype(
-        jnp.int32
-    )
-    rank = jnp.sum((jnp.cumsum(member, axis=0) - 1) * member, axis=1)
+    order = jnp.arange(tok_rows, dtype=jnp.int32)
+    earlier = (cluster_ids[:, None] == cluster_ids[None, :]) & (order[:, None] > order[None, :])
+    rank = jnp.sum(earlier.astype(jnp.int32), axis=1)
     flat = jnp.where(tail_mask, owner_ids * 4 * capacity + band_ids * capacity + rank, -1)
     dispatch = jnp.arange(tok_rows, dtype=jnp.int32)[:, None] == flat[None, :]
     dispatch_bf = dispatch.astype(jnp.bfloat16)
@@ -131,13 +130,18 @@
     )
     projections = (proj_one, proj_two, proj_three, proj_four)
     outputs = (out_one, out_two, out_three, out_four)
+    grouped = (order % slots) // capacity * (4 * capacity) + order // slots * capacity + order % capacity
+    regroup = (grouped[:, None] == order[None, :]).astype(jnp.bfloat16)
+    sorted_rows = jnp.dot(
+        regroup, recv_rows.reshape(tok_rows, width), preferred_element_type=jnp.float32
+    ).astype(jnp.bfloat16)
     band_rows = []
     band_valid = []
     band_local = []
     band_reduced = []
     band_logits = []
     for band in range(4):
-        rows = recv_rows[:, band * capacity : (band + 1) * capacity, :].reshape(slots, width)
+        rows = sorted_rows[band * slots : (band + 1) * slots]
         words = recv_words[:, band * capacity : (band + 1) * capacity].reshape(slots)
         weight_out = outputs[band][0]
         vcols = weight_out.shape[1]
@@ -191,12 +195,9 @@
         dlog = ((probs - hit) * band_valid[band][:, None].astype(jnp.float32)).astype(jnp.bfloat16)
         band_dlog.append(dlog)
         partials.append(jnp.dot(dlog, weight_out.T, preferred_element_type=jnp.float32))
-    summed = (
-        of_everyone(partials[0].astype(jnp.bfloat16), "tp").astype(jnp.float32),
-        of_everyone(partials[1].astype(jnp.bfloat16), "tp").astype(jnp.float32),
-        of_everyone(partials[2].astype(jnp.bfloat16), "tp").astype(jnp.float32),
-        of_everyone(partials[3].astype(jnp.bfloat16), "tp").astype(jnp.float32),
-    )
+    widths = [part.shape[1] for part in partials]
+    joined = of_everyone(jnp.concatenate(partials, axis=1).astype(jnp.bfloat16), "tp")
+    summed = jnp.split(joined, [sum(widths[:k]) for k in (1, 2, 3)], axis=1)
     grads_out = []
     grads_proj = []
     backs = []
@@ -223,7 +224,9 @@
     )
     tail_part = jnp.dot(dispatch_bf.T, returned, preferred_element_type=jnp.float32)
     grad_hidden = (head_mine + tail_part).astype(jnp.bfloat16)
-    grads_cat = jnp.concatenate([grad_words, grad_clus], axis=1)
+    grads_cat = jnp.concatenate(
+        [grad_words, jnp.pad(grad_clus, ((0, 0), (0, -clus_cols % 128)))], axis=1
+    )
     head_sum = lax.psum_scatter(
         jnp.dot(hidden.T, grads_cat, preferred_element_type=jnp.float32).astype(jnp.bfloat16),
         "vocab",
@@ -231,7 +234,7 @@
         tiled=True,
     ).astype(jnp.float32)
     grad_head_words = head_sum[:, :word_cols].astype(jnp.bfloat16)
-    grad_head_clusters = head_sum[:, word_cols:].astype(jnp.bfloat16)
+    grad_head_clusters = head_sum[:, word_cols : word_cols + clus_cols].astype(jnp.bfloat16)
     return (
         grad_hidden,
         grad_head_words,

time: 230 us -> 207 us (0.900)
  starting transfers between devices: 49.1 us -> 37.1 us
  local copies, waits for them, and re-layouts: 36.3 us -> 27.3 us
    all_to_all x5 -> x2, starting transfers between devices: 17.9 us -> 8.75 us  [sent_to_all(): return lax.all_to_all(copies, axis, split_axis=0, concat_axis=0, tiled=True)]
    reshape x4 -> x0, local copies, waits for them, and re-layouts: 5.42 us -> none  [body(): recv_rows[:, band * capacity:(band + 1) * capacity, :].reshape(slots, width)]
    unnamed x104 -> x93, local copies, waits for them, and re-layouts: 15.4 us -> 18.4 us
    dot_general x0 -> x1, matrix products: none -> 3.03 us  [body(): jnp.dot(regroup, recv_rows.reshape(tok_rows, width), preferred_element_ty...]
    slice x2, local copies, waits for them, and re-layouts: 5 us -> 2.1 us  [the longest x1 1.38 us: body(): rows = sorted_rows[band * slots:(band + 1) * slots]]
    all_to_all x1, starting transfers between devices: 9.49 us -> 6.66 us  [body(): lax.all_to_all(back_all, 'vocab', split_axis=0, concat_axis=0, tiled=True)]
    dot_general x4, matrix products: 4.11 us -> 1.79 us  [body(): jnp.dot(rows, projections[band][0], preferred_element_type=jnp.float32)]
    all_to_all x5 -> x2, waiting for transfers between devices: 18.3 us -> 18 us  [sent_to_all(): return lax.all_to_all(copies, axis, split_axis=0, concat_axis=0, tiled=True)]
  transfers between devices with their start and end apart: 10 -> 7, of which waited for: 8 -> 6; matrix products, arithmetic and copies ran while one was open for 24% -> 24% of each run, Pallas kernels for 0% -> 0%
where the time goes in v1:
time: 207 us; the launch traced here: 205 us
  waiting for transfers between devices  56.7 us (27%)
  matrix products  55 us (27%)
  starting transfers between devices  37.1 us (18%)
  local copies, waits for them, and re-layouts  27.3 us (13%)
  between operations  14.8 us (7%)
  other arithmetic  14.4 us (7%)
    unnamed x93, local copies, waits for them, and re-layouts  18.4 us
    all_to_all x2, waiting for transfers between devices, sent_to_all(): return lax.all_to_all(copies, axis, split_axis=0, concat_axis=0, tiled=True)  18 us
    all_to_all x1, waiting for transfers between devices, body(): lax.all_to_all(send_rows.reshape(groups, 4 * capacity, width), 'vocab', s...  17.4 us
    all_to_all x1, waiting for transfers between devices, sum_at_owner(): lax.all_to_all(parts, axis, split_axis=0, concat_axis=0, tiled=True)  10.6 us
    all_to_all x1, starting transfers between devices, body(): lax.all_to_all(send_rows.reshape(groups, 4 * capacity, width), 'vocab', s...  9.63 us
    all_to_all x2, starting transfers between devices, sent_to_all(): return lax.all_to_all(copies, axis, split_axis=0, concat_axis=0, tiled=True)  8.75 us
    dot_general x1, matrix products, body(): jnp.dot(hidden.T, grads_cat, preferred_element_type=jnp.float32)  8.75 us
    dot_general x4, matrix products, body(): jnp.dot(rows_mine.T, dred, preferred_element_type=jnp.float32)  8.15 us
  transfers between devices with their start and end apart: 7, of which 6 were waited for; matrix products, arithmetic and copies ran while one was open for 24% of the time, Pallas kernels for 0%

profile of v1, /device:TPU:1, one launch (start us, length us, event | category | flops | bytes accessed | tf_op | source)
XLA Modules:
  0.0 205.4 jit_solution(10408460267014009911)
XLA Ops:
  9.0 2.7 %convolution_convert_fusion.2 = bf16[512,2048]{1,0:T(8,128)(2,1)} fusion(bf16[512,2048]{1,0:T(8,128)(2,1)S(1)} %copy-done, s32[512]{0:T(512)S(1)} %get-tuple-element.96), kind=kOutput, calls=%fused_computation.12 | convolution fusion | flops 1075052544 | bytes 4196352 | tf_op jit(solution)/shard_map/dot_general | solution.py:111
  11.7 9.6 %all-to-all-start = ((bf16[32,16,2048]{2,1,0:T(8,128)(2,1)}), bf16[32,16,2048]{2,1,0:T(8,128)(2,1)}, u32[]{:S(2)}, u32[]{:S(2)}) async-start(bf16[32,16,2048]{2,1,0:T(8,128)(2,1)} %bitcast.151), calls=%async_computation | async-start | bytes 4194304 | tf_op jit(solution)/shard_map/all_to_all | solution.py:116
  22.1 7.0 %fusion.123 = (f32[512]{0:T(512)S(1)}, f32[512,2048]{1,0:T(8,128)S(1)}) fusion(bf16[512,2048]{1,0:T(8,128)(2,1)S(1)} %copy-done, bf16[2048,2048]{1,0:T(8,128)(2,1)} %param.16), kind=kOutput, calls=%fused_computation.232 | convolution fusion | flops 4296015360 | bytes 14682112 | tf_op jit(solution)/shard_map/dot_general | solution.py:95
  29.2 1.9 copy-done.2
  31.8 17.4 %all-to-all-done = bf16[32,16,2048]{2,1,0:T(8,128)(2,1)} async-done(((bf16[32,16,2048]{2,1,0:T(8,128)(2,1)}), bf16[32,16,2048]{2,1,0:T(8,128)(2,1)}, u32[]{:S(2)}, u32[]{:S(2)}) %all-to-all-start) | async-done | bytes 2097184 | tf_op jit(solution)/shard_map/all_to_all | solution.py:116
  49.2 3.0 %convolution_convert_fusion.1 = bf16[512,2048]{1,0:T(8,128)(2,1)S(1)} fusion(bf16[512,2048]{1,0:T(8,128)(2,1)} %bitcast.4, s32[512]{0:T(512)S(1)} %fusion.76), kind=kOutput, calls=%fused_computation.11 | convolution fusion | flops 1075052544 | bytes 4196352 | tf_op jit(solution)/shard_map/dot_general | solution.py:135
  53.6 1.6 copy-done.3
  60.8 4.2 %all-to-all-start.1 = ((f32[4,4,512]{2,1,0:T(4,128)}), f32[4,4,512]{2,1,0:T(4,128)S(1)}, u32[]{:S(2)}, u32[]{:S(2)}) async-start(f32[4,4,512]{2,1,0:T(4,128)} %broadcast_in_dim.32), calls=%async_computation.1 | async-start | bytes 65536 | tf_op jit(solution)/shard_map/all_to_all | solution.py:9
  65.0 4.3 %all-to-all-done.1 = f32[4,4,512]{2,1,0:T(4,128)S(1)} async-done(((f32[4,4,512]{2,1,0:T(4,128)}), f32[4,4,512]{2,1,0:T(4,128)S(1)}, u32[]{:S(2)}, u32[]{:S(2)}) %all-to-all-start.1) | async-done | bytes 32800 | tf_op jit(solution)/shard_map/all_to_all | solution.py:9
  69.4 4.7 %subtract_convert_fusion = bf16[512,2048]{1,0:T(8,128)(2,1)} fusion(f32[512,2048]{1,0:T(8,128)} %copy-done.2, s32[512]{0:T(512)S(1)} %get-tuple-element.95, f32[512]{0:T(512)S(1)} %bitcast.158, f32[512]{0:T(512)S(1)} %bitcast.160), kind=kLoop, calls=%fused_computation.8 | loop fusion | flops 6291456 | bytes 6297600 | tf_op jit(solution)/shard_map/convert_element_type | solution.py:180
  74.3 8.8 %fusion = bf16[2048,2176]{0,1:T(8,128)(2,1)} fusion(bf16[512,2048]{1,0:T(8,128)(2,1)S(1)} %copy-done, bf16[512,32]{1,0:T(8,128)(2,1)S(1)} %copy.55, bf16[512,2048]{1,0:T(8,128)(2,1)} %subtract_convert_fusion), kind=kOutput, calls=%fused_computation.1 | convolution fusion | flops 4574543872 | bytes 13139968 | tf_op jit(solution)/shard_map/dot_general | solution.py:231
  83.0 11.8 %copy.49 = bf16[2048,2176]{1,0:T(8,128)(2,1)} copy(bf16[2048,2176]{0,1:T(8,128)(2,1)} %fusion) | data formatting | bytes 17825792
  95.7 7.3 %all-to-all-start.3 = ((s32[32,1,16]{2,1,0:T(1,128)}), s32[32,1,16]{2,1,0:T(1,128)S(1)}, u32[]{:S(2)}, u32[]{:S(2)}) async-start(s32[32,1,16]{2,1,0:T(1,128)} %bitcast.32), calls=%async_computation.3 | async-start | bytes 32768 | tf_op jit(solution)/shard_map/all_to_all | solution.py:123
  103.0 7.0 %all-to-all-done.3 = s32[32,1,16]{2,1,0:T(1,128)S(1)} async-done(((s32[32,1,16]{2,1,0:T(1,128)}), s32[32,1,16]{2,1,0:T(1,128)S(1)}, u32[]{:S(2)}, u32[]{:S(2)}) %all-to-all-start.3) | async-done | bytes 2080 | tf_op jit(solution)/shard_map/all_to_all | solution.py:123
  114.5 1.4 broadcast_in_dim.34
  115.9 4.6 %all-to-all-start.4 = ((bf16[4,128,1920]{2,1,0:T(8,128)(2,1)}), bf16[4,128,1920]{2,1,0:T(8,128)(2,1)}, u32[]{:S(2)}, u32[]{:S(2)}) async-start(bf16[4,128,1920]{2,1,0:T(8,128)(2,1)} %broadcast_in_dim.34), calls=%async_computation.4 | async-start | bytes 3932160 | tf_op jit(solution)/shard_map/all_to_all | solution.py:9
  120.5 7.2 %fusion.125 = f32[512,2048]{1,0:T(8,128)S(1)} fusion(bf16[512,2048]{1,0:T(8,128)(2,1)S(1)} %copy-done.11, bf16[2048,2048]{1,0:T(8,128)(2,1)} %param.16), kind=kOutput, calls=%fused_computation.234 | convolution fusion | flops 4294967296 | bytes 14680064 | tf_op jit(solution)/shard_map/dot_general | solution.py:182
  128.5 1.6 copy.60
  131.2 13.7 %all-to-all-done.4 = bf16[4,128,1920]{2,1,0:T(8,128)(2,1)} async-done(((bf16[4,128,1920]{2,1,0:T(8,128)(2,1)}), bf16[4,128,1920]{2,1,0:T(8,128)(2,1)}, u32[]{:S(2)}, u32[]{:S(2)}) %all-to-all-start.4) | async-done | bytes 1966112 | tf_op jit(solution)/shard_map/all_to_all | solution.py:9
  144.9 4.8 %all-to-all-start.2 = ((bf16[4,512,512]{2,1,0:T(8,128)(2,1)}), bf16[4,512,512]{2,1,0:T(8,128)(2,1)}, u32[]{:S(2)}, u32[]{:S(2)}) async-start(bf16[4,512,512]{2,1,0:T(8,128)(2,1)} %bitcast.150), calls=%async_computation.2 | async-start | bytes 4194304 | tf_op jit(solution)/shard_map/all_to_all | solution.py:50
  153.3 1.9 reduce
  159.1 1.7 convolution_convert_fusion.16
  160.8 1.9 fusion.21
  163.8 10.6 %all-to-all-done.2 = bf16[4,512,512]{2,1,0:T(8,128)(2,1)} async-done(((bf16[4,512,512]{2,1,0:T(8,128)(2,1)}), bf16[4,512,512]{2,1,0:T(8,128)(2,1)}, u32[]{:S(2)}, u32[]{:S(2)}) %all-to-all-start.2) | async-done | bytes 2097184 | tf_op jit(solution)/shard_map/all_to_all | solution.py:50
  174.4 6.7 %all-to-all-start.5 = ((bf16[32,16,512]{2,1,0:T(8,128)(2,1)}), bf16[32,16,512]{2,1,0:T(8,128)(2,1)}, u32[]{:S(2)}, u32[]{:S(2)}) async-start(bf16[32,16,512]{2,1,0:T(8,128)(2,1)} %pad_maximum_fusion), calls=%async_computation.5 | async-start | bytes 1048576 | tf_op jit(solution)/shard_map/all_to_all | solution.py:222
  181.1 1.8 fusion.25
  182.9 2.0 fusion.14
  184.9 2.5 %fusion.12 = bf16[1,512,1024]{2,1,0:T(8,128)(2,1)} fusion(bf16[128,1920]{1,0:T(8,128)(2,1)S(1)} %reduce, bf16[128,2048]{1,0:T(8,128)(2,1)} %get-tuple-element.77, s32[]{:T(128)S(6)} %select_n.156), kind=kOutput, calls=%fused_computation.23 | convolution fusion | flops 134742016 | bytes 1441796 | tf_op jit(solution)/shard_map/dot_general | solution.py:214
  187.4 2.0 convert_reduce_fusion
  189.4 3.8 %all-to-all-done.5 = bf16[32,16,512]{2,1,0:T(8,128)(2,1)} async-done(((bf16[32,16,512]{2,1,0:T(8,128)(2,1)}), bf16[32,16,512]{2,1,0:T(8,128)(2,1)}, u32[]{:S(2)}, u32[]{:S(2)}) %all-to-all-start.5) | async-done | bytes 524320 | tf_op jit(solution)/shard_map/all_to_all | solution.py:222
  193.2 2.3 %fusion.13 = bf16[512,512]{1,0:T(8,128)(2,1)} fusion(f32[512,512]{1,0:T(8,128)S(1)} %convert_reduce_fusion, bf16[512,512]{1,0:T(8,128)(2,1)} %bitcast.44, s32[512]{0:T(512)S(1)} %get-tuple-element.96), kind=kOutput, calls=%fused_computation.25 | convolution fusion | flops 269221888 | bytes 2099200 | tf_op jit(solution)/shard_map/dot_general | solution.py:225
  196.9 1.7 slice.190
  (164 shorter events, 27.3 us)
Async XLA Ops:
  11.7 9.6 %copy-start.29 = (bf16[2048,32]{0,1:T(8,128)(2,1)S(1)}, bf16[2048,32]{0,1:T(8,128)(2,1)}, u32[]{:S(2)}) copy-start(bf16[2048,32]{0,1:T(8,128)(2,1)} %param.17) | copy-start | bytes 393220
  11.7 37.5 %all-to-all-start = ((bf16[32,16,2048]{2,1,0:T(8,128)(2,1)}), bf16[32,16,2048]{2,1,0:T(8,128)(2,1)}, u32[]{:S(2)}, u32[]{:S(2)}) async-start(bf16[32,16,2048]{2,1,0:T(8,128)(2,1)} %bitcast.151), calls=%async_computation | async-start | bytes 4194304 | tf_op jit(solution)/shard_map/all_to_all | solution.py:116
  49.2 3.0 %copy-start.34 = (bf16[1,2048,128]{2,1,0:T(8,128)(2,1)S(1)}, bf16[1,2048,128]{2,1,0:T(8,128)(2,1)}, u32[]{:S(2)}) copy-start(bf16[1,2048,128]{2,1,0:T(8,128)(2,1)} %param.21) | copy-start | bytes 1572868
  49.2 3.4 %copy-start.16 = (bf16[1,2048,256]{2,1,0:T(8,128)(2,1)S(1)}, bf16[1,2048,256]{2,1,0:T(8,128)(2,1)}, u32[]{:S(2)}) copy-start(bf16[1,2048,256]{2,1,0:T(8,128)(2,1)} %param.20) | copy-start | bytes 3145732
  49.2 3.7 %copy-start.10 = (bf16[1,2048,512]{2,1,0:T(8,128)(2,1)S(1)}, bf16[1,2048,512]{2,1,0:T(8,128)(2,1)}, u32[]{:S(2)}) copy-start(bf16[1,2048,512]{2,1,0:T(8,128)(2,1)} %param.19) | copy-start | bytes 6291460
  52.6 2.6 %copy-start.3 = (bf16[1,2048,1024]{2,1,0:T(8,128)(2,1)S(1)}, bf16[1,2048,1024]{2,1,0:T(8,128)(2,1)}, u32[]{:S(2)}) copy-start(bf16[1,2048,1024]{2,1,0:T(8,128)(2,1)} %param.18) | copy-start | bytes 12582916
  56.3 3.1 %copy-start.14 = (bf16[1,128,2048]{2,1,0:T(8,128)(2,1)S(1)}, bf16[1,128,2048]{2,1,0:T(8,128)(2,1)}, u32[]{:S(2)}) copy-start(bf16[1,128,2048]{2,1,0:T(8,128)(2,1)} %param.25) | copy-start | bytes 1572868
  56.6 3.2 %copy-start.22 = (f32[128,256]{1,0:T(8,128)}, f32[128,256]{1,0:T(8,128)S(1)}, u32[]{:S(2)}) copy-start(f32[128,256]{1,0:T(8,128)S(1)} %get-tuple-element.104) | copy-start | bytes 393220
  58.0 6.9 %copy-start.33 = (s32[512,1]{0,1:T(1,128)S(1)}, s32[512,1]{0,1:T(1,128)}, u32[]{:S(2)}) copy-start(s32[512,1]{0,1:T(1,128)} %param.14) | copy-start | bytes 6148
  60.8 8.5 %all-to-all-start.1 = ((f32[4,4,512]{2,1,0:T(4,128)}), f32[4,4,512]{2,1,0:T(4,128)S(1)}, u32[]{:S(2)}, u32[]{:S(2)}) async-start(f32[4,4,512]{2,1,0:T(4,128)} %broadcast_in_dim.32), calls=%async_computation.1 | async-start | bytes 65536 | tf_op jit(solution)/shard_map/all_to_all | solution.py:9
  64.9 130.6 %reduce-scatter.4.cloned.1.call-start = ((), (), s32[]{:S(2)}) async-start(), calls=%async_computation.7 | async-start | bytes 9191424
  94.8 15.8 %copy-start.5 = (bf16[512,2048]{1,0:T(8,128)(2,1)S(1)}, bf16[512,2048]{1,0:T(8,128)(2,1)}, u32[]{:S(2)}) copy-start(bf16[512,2048]{1,0:T(8,128)(2,1)} %copy-done.4) | copy-start | bytes 6291460
  95.7 14.3 %all-to-all-start.3 = ((s32[32,1,16]{2,1,0:T(1,128)}), s32[32,1,16]{2,1,0:T(1,128)S(1)}, u32[]{:S(2)}, u32[]{:S(2)}) async-start(s32[32,1,16]{2,1,0:T(1,128)} %bitcast.32), calls=%async_computation.3 | async-start | bytes 32768 | tf_op jit(solution)/shard_map/all_to_all | solution.py:123
  110.5 2.1 %copy-start.37 = (f32[128]{0:T(128)}, f32[128]{0:T(128)S(1)}, u32[]{:S(2)}) copy-start(f32[128]{0:T(128)S(1)} %get-tuple-element.113) | copy-start | bytes 1540
  110.6 2.6 %copy-start.41 = (f32[128]{0:T(128)}, f32[128]{0:T(128)S(1)}, u32[]{:S(2)}) copy-start(f32[128]{0:T(128)S(1)} %get-tuple-element.114) | copy-start | bytes 1540
  110.6 2.5 %copy-start.43 = (s32[128]{0:T(128)}, s32[128]{0:T(128)S(1)}, u32[]{:S(2)}) copy-start(s32[128]{0:T(128)S(1)} %get-tuple-element.116) | copy-start | bytes 1540
  110.7 2.2 %copy-start.26 = (bf16[1,512,512]{2,1,0:T(8,128)(2,1)S(1)}, bf16[1,512,512]{2,1,0:T(8,128)(2,1)}, u32[]{:S(2)}) copy-start(bf16[1,512,512]{2,1,0:T(8,128)(2,1)} %param.23) | copy-start | bytes 1572868
  115.9 4.6 %copy-start.11 = (bf16[512,2048]{1,0:T(8,128)(2,1)S(1)}, bf16[512,2048]{1,0:T(8,128)(2,1)}, u32[]{:S(2)}) copy-start(bf16[512,2048]{1,0:T(8,128)(2,1)} %subtract_convert_fusion) | copy-start | bytes 6291460
  115.9 29.0 %all-to-all-start.4 = ((bf16[4,128,1920]{2,1,0:T(8,128)(2,1)}), bf16[4,128,1920]{2,1,0:T(8,128)(2,1)}, u32[]{:S(2)}, u32[]{:S(2)}) async-start(bf16[4,128,1920]{2,1,0:T(8,128)(2,1)} %broadcast_in_dim.34), calls=%async_computation.4 | async-start | bytes 3932160 | tf_op jit(solution)/shard_map/all_to_all | solution.py:9
  120.5 7.2 %copy-start.30 = (bf16[2048,32]{0,1:T(8,128)(2,1)S(1)}, bf16[2048,32]{0,1:T(8,128)(2,1)}, u32[]{:S(2)}) copy-start(bf16[2048,32]{0,1:T(8,128)(2,1)} %param.17) | copy-start | bytes 393220
  144.9 6.0 %copy-start.18 = (bf16[128,1024]{1,0:T(8,128)(2,1)S(1)}, bf16[128,1024]{1,0:T(8,128)(2,1)}, u32[]{:S(2)}) copy-start(bf16[128,1024]{1,0:T(8,128)(2,1)} %copy-done.17) | copy-start | bytes 786436
  144.9 6.0 %copy-start.24 = (f32[128,256]{1,0:T(8,128)S(1)}, f32[128,256]{1,0:T(8,128)}, u32[]{:S(2)}) copy-start(f32[128,256]{1,0:T(8,128)} %copy-done.22) | copy-start | bytes 393220
  144.9 6.0 %copy-start.36 = (f32[128]{0:T(128)S(1)}, f32[128]{0:T(128)}, u32[]{:S(2)}) copy-start(f32[128]{0:T(128)} %copy-done.35) | copy-start | bytes 1540
  144.9 6.0 %copy-start.42 = (f32[128]{0:T(128)S(1)}, f32[128]{0:T(128)}, u32[]{:S(2)}) copy-start(f32[128]{0:T(128)} %copy-done.41) | copy-start | bytes 1540
  144.9 6.0 %copy-start.44 = (s32[128]{0:T(128)S(1)}, s32[128]{0:T(128)}, u32[]{:S(2)}) copy-start(s32[128]{0:T(128)} %copy-done.43) | copy-start | bytes 1540
  144.9 7.2 %copy-start.21 = (f32[128,512]{1,0:T(8,128)S(1)}, f32[128,512]{1,0:T(8,128)}, u32[]{:S(2)}) copy-start(f32[128,512]{1,0:T(8,128)} %copy-done.19) | copy-start | bytes 786436
  144.9 7.2 %copy-start.32 = (bf16[128,512]{1,0:T(8,128)(2,1)S(1)}, bf16[128,512]{1,0:T(8,128)(2,1)}, u32[]{:S(2)}) copy-start(bf16[128,512]{1,0:T(8,128)(2,1)} %copy-done.31) | copy-start | bytes 393220
  144.9 7.2 %copy-start.38 = (f32[128]{0:T(128)S(1)}, f32[128]{0:T(128)}, u32[]{:S(2)}) copy-start(f32[128]{0:T(128)} %copy-done.37) | copy-start | bytes 1540
  144.9 7.2 %copy-start.40 = (s32[128]{0:T(128)S(1)}, s32[128]{0:T(128)}, u32[]{:S(2)}) copy-start(s32[128]{0:T(128)} %copy-done.39) | copy-start | bytes 1540
  144.9 29.5 %all-to-all-start.2 = ((bf16[4,512,512]{2,1,0:T(8,128)(2,1)}), bf16[4,512,512]{2,1,0:T(8,128)(2,1)}, u32[]{:S(2)}, u32[]{:S(2)}) async-start(bf16[4,512,512]{2,1,0:T(8,128)(2,1)} %bitcast.150), calls=%async_computation.2 | async-start | bytes 4194304 | tf_op jit(solution)/shard_map/all_to_all | solution.py:50
  174.4 18.8 %all-to-all-start.5 = ((bf16[32,16,512]{2,1,0:T(8,128)(2,1)}), bf16[32,16,512]{2,1,0:T(8,128)(2,1)}, u32[]{:S(2)}, u32[]{:S(2)}) async-start(bf16[32,16,512]{2,1,0:T(8,128)(2,1)} %pad_maximum_fusion), calls=%async_computation.5 | async-start | bytes 1048576 | tf_op jit(solution)/shard_map/all_to_all | solution.py:222
  184.9 13.7 %copy-start.1 = (bf16[512,2048]{1,0:T(8,128)(2,1)S(1)}, bf16[512,2048]{1,0:T(8,128)(2,1)}, u32[]{:S(2)}) copy-start(bf16[512,2048]{1,0:T(8,128)(2,1)} %param.13) | copy-start | bytes 6291460
  (20 other events, 29.6 us)
Sparse Core Ops, SparseCore 0:
  94.9 90.4 reduce-scatter.3
